TPU v7x, 32 devices: a whole 2x2x4 slice. The times are simulated.
32 devices in a mesh: groups: 2 (over x), ctx: 4 (over y, core), head: 4 (over z).
Axes of the slice: x: 2, y: 2, z: 4, core: 2. Of those that a mesh axis runs over, the one named last changes fastest.
Arguments:
- queries: bfloat16 [256, 16384], P(('groups', 'ctx'), 'head'), parts along dimension 0, may hold values from -8 to 8
- cache_keys: bfloat16 [16384, 1024], P(('groups', 'ctx'), 'head'), parts along dimension 0, may hold values from -6 to 6
- cache_values: bfloat16 [16384, 1024], P(('groups', 'ctx'), 'head'), parts along dimension 0, may hold values from -6 to 6
- new_keys: bfloat16 [256, 1024], P(('groups', 'ctx'), 'head'), parts along dimension 0, may hold values from -8 to 8
- new_values: bfloat16 [256, 1024], P(('groups', 'ctx'), 'head'), parts along dimension 0, may hold values from -6 to 6
- out_weight: bfloat16 [16384, 16384], P('head', 'ctx'), may hold values from -0.1796875 to 0.1796875
- new_counts: int32 [8, 4], P('groups'), parts along dimension 0, may hold values from 1 to 16, 32 in all within a row
- cache_counts: int32 [8, 4], P('groups'), parts along dimension 0, may hold values from 1 to 512, 1536 in all within a row
- row_dest: int32 [256], P('groups'), parts along dimension 0, may hold values from 0 to 127, each once
Outputs:
- projected: bfloat16 [256, 16384], P(('groups', 'head'), 'ctx'), parts along dimension 0
There are 2 independent parts, one for each index of `groups`. A program takes and returns all parts, laid end to end along the dimension named above; an argument that names none is the same for every part. Nothing has to cross between parts.
Inputs may be any that keep to these rules, and one draw needn't show every extreme that they name: Each row of new_counts sums to 32. `cache_counts`: each shard's counts sum to 1536. `row_dest`: each output row is named once.
All inputs are finite; a program needn't handle non-finite values.
Results may differ from a plain program's by a relative error of at most 0.017.
Values may be sent and summed in bfloat16 or wider, within the bound.
A program may use at most 128 MiB of HBM per device.

v0:
```python
import functools
import math

import jax
import jax.numpy as jnp
from jax import lax
from jax.experimental import pallas as pl
from jax.experimental.pallas import tpu as pltpu
from jax.sharding import PartitionSpec as P

HEAD_DIM = 128
NEG = -1e30
MESH = pl.DeviceIdType.MESH
F32 = jnp.float32
BF16 = jnp.bfloat16


def tiles_of(total, width):
    return [(at, min(width, total - at)) for at in range(0, total, width)]


def fused(
    n, nh, q_ref, ck_ref, cv_ref, nk_ref, nv_ref, w_ref, ncnt, ccnt, rd_ref, out_ref,
    q_all, kbuf, vbuf, bias, s_scr, part, stat, rpart, rstat, att, order, wbuf, ybuf, rbuf, rpair,
    k_sem, v_sem, w_sem, own_sem, q_send, q_recv, p_send, p_recv, t_send, t_recv,
    a_send, a_recv, y_send, y_recv, f_recv,
):
    me = lax.axis_index("ctx")
    hz = lax.axis_index("head")
    core = lax.rem(me, 2)
    chip = lax.div(me, 2)
    chips = n // 2
    mate = chip * 2 + 1 - core
    rows = q_ref.shape[0]
    cached = ck_ref.shape[0]
    keys = kbuf.shape[0]
    kv = ck_ref.shape[1] // HEAD_DIM
    grp = q_ref.shape[1] // HEAD_DIM // kv
    wide = grp * HEAD_DIM
    reqs = ncnt.shape[1]
    chunks, depth, cw = wbuf.shape
    orows = out_ref.shape[0]
    scale = 1.0 / math.sqrt(HEAD_DIM)
    scale2 = scale * math.log2(math.e)

    own = pltpu.make_async_copy(q_ref, q_all.at[me], own_sem)
    own.start()
    kcopies = [
        pltpu.make_async_copy(ck_ref, kbuf.at[pl.ds(0, cached)], k_sem.at[0]),
        pltpu.make_async_copy(nk_ref, kbuf.at[pl.ds(cached, rows)], k_sem.at[1]),
    ]
    for h in range(kv):
        cols = pl.ds(h * HEAD_DIM, HEAD_DIM)
        kcopies.append(pltpu.make_async_copy(
            cv_ref.at[:, cols], vbuf.at[h, pl.ds(0, cached), pl.ds(0, HEAD_DIM)], v_sem.at[h, 0]))
        kcopies.append(pltpu.make_async_copy(
            nv_ref.at[:, cols], vbuf.at[h, pl.ds(cached, rows), pl.ds(0, HEAD_DIM)], v_sem.at[h, 1]))
    for copy in kcopies:
        copy.start()

    barrier = pltpu.get_barrier_semaphore()
    for d in range(1, n):
        pl.semaphore_signal(barrier, inc=1, device_id={"ctx": lax.rem(me + d, n)}, device_id_type=MESH)
    for d in range(1, nh):
        pl.semaphore_signal(barrier, inc=1, device_id={"head": lax.rem(hz + d, nh)}, device_id_type=MESH)

    def wcopy(c):
        return pltpu.make_async_copy(
            w_ref.at[:, pl.ds(pl.multiple_of(c * cw, cw), cw)], wbuf.at[c], w_sem.at[c])

    pad = keys - cached - rows
    kbuf[pl.ds(cached + rows, pad), :] = jnp.zeros((pad, kbuf.shape[1]), BF16)
    for h in range(kv):
        vbuf[h, pl.ds(cached + rows, pad), pl.ds(0, HEAD_DIM)] = jnp.zeros((pad, HEAD_DIM), BF16)
        vbuf[h, :, pl.ds(HEAD_DIM, HEAD_DIM)] = jnp.ones((keys, HEAD_DIM), BF16)

    pl.semaphore_wait(barrier, n - 1 + nh - 1)

    def gather_copy(src, dst, send, recv, to):
        return pltpu.make_async_remote_copy(
            src_ref=src, dst_ref=dst, send_sem=send, recv_sem=recv,
            device_id={"ctx": to}, device_id_type=MESH)

    def q_out(k):
        to = lax.rem(chip + chips - k, chips) * 2 + core
        return gather_copy(q_ref, q_all.at[me], q_send.at[2 * k], q_recv.at[2 * k], to)

    q_mate = gather_copy(q_ref, q_all.at[me], q_send.at[1], q_recv.at[1], mate)
    for k in range(1, chips):
        q_out(k).start()
    q_mate.start()

    def block_of(i):
        return lax.rem(chip + lax.div(i, 2), chips) * 2 + lax.rem(core + i, 2)

    def q_in(i):
        b = block_of(i)
        return gather_copy(q_all.at[b], q_all.at[b], q_send.at[i], q_recv.at[i], mate)

    def q_pass(i):
        b = block_of(i)
        return gather_copy(q_all.at[b], q_all.at[b], q_send.at[i + 1], q_recv.at[i + 1], mate)

    def start_w(c, _):
        wcopy(c).start()
        return 0

    lax.fori_loop(0, chunks, start_w, 0)

    lane = lax.broadcasted_iota(jnp.int32, (1, keys), 1)
    key_req = jnp.zeros((1, keys), jnp.int32)
    edge = jnp.int32(0)
    for r in range(reqs):
        edge = edge + ccnt[me, r]
        key_req = key_req + (lane >= edge).astype(jnp.int32)
    fresh = lane - cached
    fresh_req = jnp.zeros((1, keys), jnp.int32)
    edge = jnp.int32(0)
    for r in range(reqs):
        edge = edge + ncnt[me, r]
        fresh_req = fresh_req + (fresh >= edge).astype(jnp.int32)
    key_req = jnp.where(lane >= cached, jnp.where(fresh < rows, fresh_req, -1), key_req)
    key_pos = jnp.where(lane >= cached, me * rows + fresh, -1)

    for copy in kcopies:
        copy.wait()
    own.wait()

    def part_copy(b, h, slot, to):
        cols = pl.ds(h * wide, wide)
        return gather_copy(part.at[b, :, cols], rpart.at[slot, :, cols],
                           p_send.at[b, h], p_recv.at[slot, h], to)

    def stat_copy(b, h, slot, to):
        return gather_copy(stat.at[b, h], rstat.at[slot, h], t_send.at[b, h], t_recv.at[slot, h], to)

    def send_share(b, h, slot, to):
        stat_copy(b, h, slot, to).start()
        part_copy(b, h, slot, to).start()

    def wait_share(slot, h):
        stat_copy(slot, h, slot, mate).wait_recv()
        part_copy(slot, h, slot, mate).wait_recv()

    def blend(b, h, slots, out):
        stats = [stat[b, h]] + [rstat[slot, h] for slot in slots]
        best = functools.reduce(jnp.maximum, stats)
        weights = [jnp.exp(item - best) for item in stats]
        whole = functools.reduce(jnp.add, weights)
        weights = [item / whole for item in weights]
        for g in range(grp):
            at = (h * grp + g) * HEAD_DIM
            mixed = None
            for j, weight in enumerate(weights):
                piece = part[b, :, at:at + HEAD_DIM] if j == 0 else rpart[slots[j - 1], :, at:at + HEAD_DIM]
                term = jnp.broadcast_to(weight[:, g:g + 1], (rows, HEAD_DIM)) * piece.astype(F32)
                mixed = term if mixed is None else mixed + term
            out[b, :, at:at + HEAD_DIM] = mixed.astype(BF16)
        return best + jnp.log(whole)

    spans = tiles_of(keys, 512)
    lane128 = lax.broadcasted_iota(jnp.int32, (rows, HEAD_DIM), 1)

    def step(i, _):
        b = block_of(i)

        @pl.when(i > 0)
        def _():
            q_in(i).wait_recv()

        @pl.when((i > 0) & (lax.rem(i, 2) == 0))
        def _():
            q_pass(i).start()

        row = lax.broadcasted_iota(jnp.int32, (rows, 1), 0)
        row_req = jnp.zeros((rows, 1), jnp.int32)
        edge = jnp.int32(0)
        for r in range(reqs):
            edge = edge + ncnt[b, r]
            row_req = row_req + (row >= edge).astype(jnp.int32)
        seen = (key_req == row_req) & (key_pos <= b * rows + row)
        bias[...] = jnp.where(seen, 0.0, NEG)

        for h in range(kv):
            q = jnp.concatenate(
                [q_all[b, :, (h * grp + g) * HEAD_DIM:(h * grp + g + 1) * HEAD_DIM] for g in range(grp)], axis=0)
            most = None
            for at, size in spans:
                s = lax.dot_general(
                    q, kbuf[at:at + size, h * HEAD_DIM:(h + 1) * HEAD_DIM],
                    (((1,), (1,)), ((), ())), preferred_element_type=F32)
                s = (s.reshape(grp, rows, size) + bias[:, at:at + size][None]).reshape(grp * rows, size)
                s_scr[h, :, at:at + size] = s
                for j in range(0, size, HEAD_DIM):
                    piece = s[:, j:j + HEAD_DIM]
                    most = piece if most is None else jnp.maximum(most, piece)
            top = jnp.max(most, axis=1, keepdims=True)
            shift = top * scale2
            acc = None
            for at, size in spans:
                p = jnp.exp2(s_scr[h, :, at:at + size] * scale2 - shift).astype(BF16)
                term = jnp.dot(p, vbuf[h, at:at + size, :], preferred_element_type=F32)
                acc = term if acc is None else acc + term
            total = acc[:, HEAD_DIM:]
            value = (acc[:, :HEAD_DIM] / jnp.maximum(total, 1.0)).astype(BF16)
            lse = jnp.where(top > 0.5 * NEG, top * scale + jnp.log(jnp.maximum(total, 1.0)), NEG)
            packed = jnp.zeros((rows, HEAD_DIM), F32)
            for g in range(grp):
                at = (h * grp + g) * HEAD_DIM
                part[b, :, at:at + HEAD_DIM] = value[g * rows:(g + 1) * rows]
                packed = jnp.where(lane128 == g, lse[g * rows:(g + 1) * rows], packed)
            stat[b, h] = packed

        for h in range(kv):
            @pl.when(i == 1)
            def _():
                send_share(b, h, me, mate)

            @pl.when((i > 1) & (lax.rem(i, 2) == 0))
            def _():
                send_share(b, h, block_of(i + 1), mate)

            @pl.when((i > 1) & (lax.rem(i, 2) == 1))
            def _():
                slot = block_of(i - 1)
                wait_share(slot, h)
                stat[b, h] = blend(b, h, [slot], part)
                send_share(b, h, me, b)
        return 0

    lax.fori_loop(0, n, step, 0)

    def a_out(h, k):
        cols = pl.ds(h * wide, wide)
        to = lax.rem(chip + chips - k, chips) * 2 + core
        return gather_copy(att.at[me, :, cols], att.at[me, :, cols],
                           a_send.at[h, 2 * k], a_recv.at[h, 2 * k], to)

    def a_mate(h):
        cols = pl.ds(h * wide, wide)
        return gather_copy(att.at[me, :, cols], att.at[me, :, cols],
                           a_send.at[h, 1], a_recv.at[h, 1], mate)

    def a_in(h, i):
        cols = pl.ds(h * wide, wide)
        b = block_of(jnp.int32(i))
        return gather_copy(att.at[b, :, cols], att.at[b, :, cols],
                           a_send.at[h, i], a_recv.at[h, i], mate)

    def a_pass(h, i):
        cols = pl.ds(h * wide, wide)
        b = block_of(jnp.int32(i))
        return gather_copy(att.at[b, :, cols], att.at[b, :, cols],
                           a_send.at[h, i + 1], a_recv.at[h, i + 1], mate)

    for h in range(kv):
        slots = [mate] + [lax.rem(chip + k, chips) * 2 + 1 - core for k in range(1, chips)]
        for slot in slots:
            wait_share(slot, h)
        blend(me, h, slots, att)
        for k in range(1, chips):
            a_out(h, k).start()
        a_mate(h).start()

    for h in range(kv):
        for k in range(1, chips):
            a_in(h, 2 * k).wait_recv()
            a_pass(h, 2 * k).start()
    for h in range(kv):
        for k in range(chips):
            a_in(h, 2 * k + 1).wait_recv()

    everyone = n * rows
    pick = (lax.broadcasted_iota(jnp.int32, (everyone, everyone), 0) == rd_ref[...]).astype(F32).astype(BF16)
    for at, size in tiles_of(att.shape[2], 1024):
        order[:, at:at + size] = jnp.dot(
            pick, att[:, :, at:at + size].reshape(everyone, size), preferred_element_type=F32).astype(BF16)

    first = lax.div(hz, 2) * 2
    even = lax.rem(hz, 2) == 0
    other = first + 1 - lax.rem(hz, 2)

    def columns(c):
        return pl.ds(pl.multiple_of(c * cw, cw), cw)

    def share(t):
        return pl.ds(t * orows, orows)

    def to_pair(c, t):
        return pltpu.make_async_remote_copy(
            src_ref=ybuf.at[share(t), columns(c)], dst_ref=rpair.at[t, :, columns(c)],
            send_sem=y_send.at[t, c], recv_sem=y_recv.at[t, c],
            device_id={"head": other}, device_id_type=MESH)

    def to_owner(c, t):
        return pltpu.make_async_remote_copy(
            src_ref=ybuf.at[share(t), columns(c)], dst_ref=rbuf.at[lax.div(hz, 2), :, columns(c)],
            send_sem=y_send.at[t, c], recv_sem=f_recv.at[lax.div(hz, 2), c],
            device_id={"head": t}, device_id_type=MESH)

    def from_pair(c, p):
        return pltpu.make_async_remote_copy(
            src_ref=rbuf.at[p, :, columns(c)], dst_ref=rbuf.at[p, :, columns(c)],
            send_sem=y_send.at[hz, c], recv_sem=f_recv.at[p, c],
            device_id={"head": other}, device_id_type=MESH)

    def hands_over(t):
        return (t == other) | ((t > first + 1) & even) | ((t < first) & jnp.logical_not(even))

    def carries(t):
        return ((t > first + 1) & jnp.logical_not(even)) | ((t < first) & even)

    def project(c, _):
        @pl.when(c < chunks)
        def _():
            wcopy(c).wait()
            y = jnp.dot(order[...], wbuf[c], preferred_element_type=F32)
            ybuf[:, columns(c)] = y.astype(BF16)
            for t in range(nh):
                @pl.when(hands_over(t))
                def _():
                    to_pair(c, t).start()

        @pl.when(c >= lag)
        def _():
            for t in range(nh):
                @pl.when(carries(t))
                def _():
                    to_pair(c - lag, t).wait_recv()
                    cols = columns(c - lag)
                    ybuf[share(t), cols] = (
                        ybuf[share(t), cols].astype(F32) + rpair[t, :, cols].astype(F32)).astype(BF16)
                    to_owner(c - lag, t).start()
        return 0

    lag = min(4, chunks)
    lax.fori_loop(0, chunks + lag, project, 0)

    def finish(c, _):
        cols = columns(c)
        to_pair(c, hz).wait_recv()
        total = ybuf[pl.ds(pl.multiple_of(hz * orows, orows), orows), cols].astype(F32) + rpair[hz, :, cols].astype(F32)
        for step_pair in range(1, nh // 2):
            p = lax.rem(lax.div(hz, 2) + step_pair, nh // 2)
            from_pair(c, p).wait_recv()
            total = total + rbuf[p, :, cols].astype(F32)
        out_ref[:, cols] = total.astype(BF16)
        return 0

    lax.fori_loop(0, chunks, finish, 0)

    for k in range(1, chips):
        q_out(k).wait_send()
        q_pass(jnp.int32(2 * k)).wait_send()
    q_mate.wait_send()

    def drain(i, _):
        b = block_of(i)
        for h in range(kv):
            stat_copy(b, h, me, mate).wait_send()
            part_copy(b, h, me, mate).wait_send()
        return 0

    lax.fori_loop(1, n, drain, 0)
    for h in range(kv):
        a_mate(h).wait_send()
        for k in range(1, chips):
            a_out(h, k).wait_send()
            a_pass(h, 2 * k).wait_send()

    def drain_y(c, _):
        for t in range(nh):
            @pl.when(t != hz)
            def _():
                to_pair(c, t).wait_send()
        return 0

    lax.fori_loop(0, chunks, drain_y, 0)


def per_device(
    n, nh, queries, cache_keys, cache_values, new_keys, new_values, out_weight,
    new_counts, cache_counts, row_dest,
):
    rows, width = queries.shape
    cached, kvw = cache_keys.shape
    kv = kvw // HEAD_DIM
    grp = width // kvw
    depth, cols = out_weight.shape
    keys = cached + -(-rows // HEAD_DIM) * HEAD_DIM
    everyone = n * rows
    orows = everyone // nh
    cw = 1024 if cols % 1024 == 0 else HEAD_DIM
    chunks = cols // cw
    dma = pltpu.SemaphoreType.DMA
    hbm = pl.BlockSpec(memory_space=pl.ANY)
    smem = pl.BlockSpec(memory_space=pltpu.SMEM)
    vmem = pl.BlockSpec(memory_space=pltpu.VMEM)
    return pl.pallas_call(
        functools.partial(fused, n, nh),
        out_shape=jax.ShapeDtypeStruct((orows, cols), BF16),
        in_specs=[hbm] * 6 + [smem] * 2 + [vmem],
        out_specs=vmem,
        scratch_shapes=[
            pltpu.VMEM((n, rows, width), BF16),
            pltpu.VMEM((keys, kvw), BF16),
            pltpu.VMEM((kv, keys, 2 * HEAD_DIM), BF16),
            pltpu.VMEM((rows, keys), F32),
            pltpu.VMEM((kv, grp * rows, keys), F32),
            pltpu.VMEM((n, rows, width), BF16),
            pltpu.VMEM((n, kv, rows, HEAD_DIM), F32),
            pltpu.VMEM((n, rows, width), BF16),
            pltpu.VMEM((n, kv, rows, HEAD_DIM), F32),
            pltpu.VMEM((n, rows, width), BF16),
            pltpu.VMEM((everyone, width), BF16),
            pltpu.VMEM((chunks, depth, cw), BF16),
            pltpu.VMEM((everyone, cols), BF16),
            pltpu.VMEM((nh // 2, orows, cols), BF16),
            pltpu.VMEM((nh, orows, cols), BF16),
            dma((2,)), dma((kv, 2)), dma((chunks,)), dma,
            dma((n,)), dma((n,)),
            dma((n, kv)), dma((n, kv)), dma((n, kv)), dma((n, kv)),
            dma((kv, n)), dma((kv, n)),
            dma((nh, chunks)), dma((nh, chunks)), dma((nh // 2, chunks)),
        ],
        compiler_params=pltpu.CompilerParams(
            collective_id=0, has_side_effects=True, vmem_limit_bytes=60 * 1024 * 1024),
    )(queries, cache_keys, cache_values, new_keys, new_values, out_weight,
      new_counts, cache_counts, row_dest.reshape(1, everyone))


def solution(mesh):
    n, nh = mesh.shape["ctx"], mesh.shape["head"]
    return jax.shard_map(
        functools.partial(per_device, n, nh),
        mesh=mesh,
        in_specs=(
            P(("groups", "ctx"), "head"),
            P(("groups", "ctx"), "head"),
            P(("groups", "ctx"), "head"),
            P(("groups", "ctx"), "head"),
            P(("groups", "ctx"), "head"),
            P("head", "ctx"),
            P("groups", None),
            P("groups", None),
            P("groups"),
        ),
        out_specs=P(("groups", "head"), "ctx"),
        check_vma=False,
    )
```

profile of v0, /device:TPU:0, one launch (start us, length us, event | category | flops | bytes accessed | tf_op | source)
XLA Modules:
  0.0 59.2 jit_solution(6680368268250193229)
XLA Ops:
  0.0 57.5 %shard_map.91 = bf16[32,4096]{1,0:T(8,128)(2,1)} custom-call(bf16[32,4096]{1,0:T(8,128)(2,1)} %q_ref.1, bf16[2048,256]{1,0:T(8,128)(2,1)} %ck_ref.1, bf16[2048,256]{1,0:T(8,128)(2,1)} %cv_ref.1, bf16[32,256]{1,0:T(8,128)(2,1)} %nk_ref.1, bf16[32,256]{1,0:T(8,128)(2,1)} %nv_ref.1, bf16[4096,4096]{1,0:T(8,128)(2,1)} %w_ref.1, s32[4,4]{1,0:T(4,128)} %ncnt.1, ...), custom_call_target="tpu_custom_call" | custom-call | tf_op jit(solution)/shard_map/pallas_call | solution.py:399
  57.5 1.7 %copy.11 = bf16[32,4096]{1,0:T(8,128)(2,1)} copy(bf16[32,4096]{1,0:T(8,128)(2,1)} %shard_map.91) | data formatting | bytes 524288
where the time goes:
time: 59.3 us; the launch traced here: 59.2 us
  Pallas kernels  57.5 us (97%)
  local copies, waits for them, and re-layouts  1.67 us (3%)
    pallas_call x1, Pallas kernels, per_device(): pl.pallas_call(functools.partial(fused, n, nh), out_shape=jax.ShapeDtypeS...  57.5 us
    unnamed x1, local copies, waits for them, and re-layouts  1.67 us

commit v1 on v0

v1 whole, which is shorter than its diff:
```python
import functools
import math

import jax
import jax.numpy as jnp
from jax import lax
from jax.experimental import pallas as pl
from jax.experimental.pallas import tpu as pltpu
from jax.sharding import PartitionSpec as P

HEAD_DIM = 128
NEG = -1e30
MESH = pl.DeviceIdType.MESH
F32 = jnp.float32
BF16 = jnp.bfloat16


def tiles_of(total, width):
    return [(at, min(width, total - at)) for at in range(0, total, width)]


def parts_of(kv, grp):
    if kv % 2 == 0:
        return [[(h, 0, grp) for h in range(s * kv // 2, (s + 1) * kv // 2)] for s in range(2)]
    return [[(0, s * grp // 2, (s + 1) * grp // 2)] for s in range(2)]


def fused(
    n, nh, q_ref, ck_ref, cv_ref, nk_ref, nv_ref, w_ref, ncnt, ccnt, rd_ref, out_ref,
    q_all, kbuf, vbuf, bias, s_scr, part, stat, mpart, mstat, comb, cstat, xpart, xstat,
    att, order, wbuf, ybuf, rbuf, obuf,
    k_sem, v_sem, w_sem, own_sem, q_send, q_recv, m_send, m_recv, ms_send, ms_recv,
    x_send, x_recv, xs_send, xs_recv, a_send, a_recv, y_send, y_recv, o_sem,
):
    me = lax.axis_index("ctx")
    hz = lax.axis_index("head")
    core = lax.rem(me, 2)
    chip = lax.div(me, 2)
    chips = n // 2
    mate = chip * 2 + 1 - core
    rows = q_ref.shape[0]
    cached = ck_ref.shape[0] * 3 // 4
    keys = kbuf.shape[0]
    kv = ck_ref.shape[1] // HEAD_DIM
    grp = q_ref.shape[1] // HEAD_DIM // kv
    half = part.shape[3]
    heads = half // HEAD_DIM
    bands = rows // 8
    reqs = ncnt.shape[1]
    chunks, depth, cw = wbuf.shape
    orows = out_ref.shape[0]
    scale = 1.0 / math.sqrt(HEAD_DIM)
    scale2 = scale * math.log2(math.e)
    above = jnp.minimum(hz + 1, nh - 1)
    below = jnp.maximum(hz - 1, 0)

    barrier = pltpu.get_barrier_semaphore()
    pl.semaphore_signal(barrier, inc=1, device_id={"ctx": mate}, device_id_type=MESH)
    for d in range(1, chips):
        pl.semaphore_signal(
            barrier, inc=1, device_id={"ctx": lax.rem(me + 2 * d, n)}, device_id_type=MESH)

    @pl.when(hz < nh - 1)
    def _():
        pl.semaphore_signal(barrier, inc=1, device_id={"head": above}, device_id_type=MESH)

    @pl.when(hz > 0)
    def _():
        pl.semaphore_signal(barrier, inc=1, device_id={"head": below}, device_id_type=MESH)

    own = pltpu.make_async_copy(q_ref, q_all.at[me], own_sem)
    own.start()
    kcopies = [
        pltpu.make_async_copy(ck_ref.at[pl.ds(0, cached)], kbuf.at[pl.ds(0, cached)], k_sem.at[0]),
        pltpu.make_async_copy(nk_ref, kbuf.at[pl.ds(cached, rows)], k_sem.at[1]),
    ]
    for h in range(kv):
        cols = pl.ds(h * HEAD_DIM, HEAD_DIM)
        kcopies.append(pltpu.make_async_copy(
            cv_ref.at[pl.ds(0, cached), cols], vbuf.at[h, pl.ds(0, cached), pl.ds(0, HEAD_DIM)],
            v_sem.at[h, 0]))
        kcopies.append(pltpu.make_async_copy(
            nv_ref.at[:, cols], vbuf.at[h, pl.ds(cached, rows), pl.ds(0, HEAD_DIM)], v_sem.at[h, 1]))
    for copy in kcopies:
        copy.start()

    def wcopy(c):
        return pltpu.make_async_copy(
            w_ref.at[:, pl.ds(pl.multiple_of(c * cw, cw), cw)], wbuf.at[c], w_sem.at[c])

    pad = keys - cached - rows
    kbuf[pl.ds(cached + rows, pad), :] = jnp.zeros((pad, kbuf.shape[1]), BF16)
    for h in range(kv):
        vbuf[h, pl.ds(cached + rows, pad), pl.ds(0, HEAD_DIM)] = jnp.zeros((pad, HEAD_DIM), BF16)
        vbuf[h, :, pl.ds(HEAD_DIM, HEAD_DIM)] = jnp.ones((keys, HEAD_DIM), BF16)

    pl.semaphore_wait(
        barrier, chips + (hz < nh - 1).astype(jnp.int32) + (hz > 0).astype(jnp.int32))

    def to_ctx(src, dst, send, recv, to):
        return pltpu.make_async_remote_copy(
            src_ref=src, dst_ref=dst, send_sem=send, recv_sem=recv,
            device_id={"ctx": to}, device_id_type=MESH)

    def twin(d):
        return lax.rem(chip + d, chips) * 2 + core

    def q_out(k):
        return to_ctx(q_ref, q_all.at[me], q_send.at[2 * k], q_recv.at[2 * k], twin(chips - k))

    q_mate = to_ctx(q_ref, q_all.at[me], q_send.at[1], q_recv.at[1], mate)
    for k in range(1, chips):
        q_out(k).start()
    q_mate.start()

    def block_of(i):
        return lax.rem(chip + lax.div(i, 2), chips) * 2 + lax.rem(core + i, 2)

    def q_in(i):
        b = block_of(i)
        return to_ctx(q_all.at[b], q_all.at[b], q_send.at[i], q_recv.at[i], mate)

    def q_pass(i):
        b = block_of(i)
        return to_ctx(q_all.at[b], q_all.at[b], q_send.at[i + 1], q_recv.at[i + 1], mate)

    def start_w(c, _):
        wcopy(c).start()
        return 0

    lax.fori_loop(0, chunks, start_w, 0)

    lane = lax.broadcasted_iota(jnp.int32, (1, keys), 1)
    key_req = jnp.zeros((1, keys), jnp.int32)
    edge = jnp.int32(0)
    for r in range(reqs):
        edge = edge + ccnt[me, r]
        key_req = key_req + (lane >= edge).astype(jnp.int32)
    fresh = lane - cached
    fresh_req = jnp.zeros((1, keys), jnp.int32)
    edge = jnp.int32(0)
    for r in range(reqs):
        edge = edge + ncnt[me, r]
        fresh_req = fresh_req + (fresh >= edge).astype(jnp.int32)
    key_req = jnp.where(lane >= cached, jnp.where(fresh < rows, fresh_req, -1), key_req)
    key_pos = jnp.where(lane >= cached, me * rows + fresh, -1)

    for copy in kcopies:
        copy.wait()
    own.wait()

    def mate_part(b):
        return to_ctx(part.at[b, 1 - core], mpart.at[b], m_send.at[b], m_recv.at[b], mate)

    def mate_stat(b):
        return to_ctx(stat.at[b, 1 - core], mstat.at[b], ms_send.at[b], ms_recv.at[b], mate)

    def chip_part(b, d):
        return to_ctx(comb.at[b], xpart.at[d - 1, b], x_send.at[d - 1, b], x_recv.at[d - 1, b], twin(d))

    def chip_stat(b, d):
        return to_ctx(cstat.at[b], xstat.at[d - 1, b], xs_send.at[d - 1, b], xs_recv.at[d - 1, b], twin(d))

    def att_part(b, side):
        return to_ctx(att.at[b, side], att.at[b, side], a_send.at[b], a_recv.at[b], mate)

    def spread(weight, e):
        return jnp.concatenate(
            [jnp.broadcast_to(weight[:, r * heads + e:r * heads + e + 1], (8, HEAD_DIM))
             for r in range(bands)], axis=0)

    def blend(pieces, stats, store):
        best = functools.reduce(jnp.maximum, stats)
        weights = [jnp.exp(item - best) for item in stats]
        whole = functools.reduce(jnp.add, weights)
        weights = [item / whole for item in weights]
        for e in range(heads):
            cols = slice(e * HEAD_DIM, (e + 1) * HEAD_DIM)
            terms = [spread(w, e) * piece[:, cols].astype(F32) for w, piece in zip(weights, pieces)]
            store(cols, functools.reduce(jnp.add, terms).astype(BF16))
        return best + jnp.log(whole)

    def combine(b):
        mate_stat(b).wait_recv()
        mate_part(b).wait_recv()

        def store(cols, value):
            comb[b, :, cols] = value

        cstat[b] = blend([part.at[b, core], mpart.at[b]], [stat[b, core], mstat[b]], store)
        for d in range(1, chips):
            chip_stat(b, d).start()
            chip_part(b, d).start()

    def conclude(b):
        for d in range(1, chips):
            chip_stat(b, d).wait_recv()
            chip_part(b, d).wait_recv()

        def store(cols, value):
            att[b, core, :, cols] = value

        blend([comb.at[b]] + [xpart.at[d - 1, b] for d in range(1, chips)],
              [cstat[b]] + [xstat[d - 1, b] for d in range(1, chips)], store)
        att_part(b, core).start()

    spans = tiles_of(keys, 512)
    band_lane = lax.broadcasted_iota(jnp.int32, (8, HEAD_DIM), 1)

    def step(i, _):
        b = block_of(i)

        @pl.when(i > 0)
        def _():
            q_in(i).wait_recv()

        @pl.when((i > 0) & (lax.rem(i, 2) == 0))
        def _():
            q_pass(i).start()

        row = lax.broadcasted_iota(jnp.int32, (rows, 1), 0)
        row_req = jnp.zeros((rows, 1), jnp.int32)
        edge = jnp.int32(0)
        for r in range(reqs):
            edge = edge + ncnt[b, r]
            row_req = row_req + (row >= edge).astype(jnp.int32)
        seen = (key_req == row_req) & (key_pos <= b * rows + row)
        bias[...] = jnp.where(seen, 0.0, NEG)

        slot = 0
        for side, items in enumerate(parts_of(kv, grp)):
            packed = jnp.zeros((8, HEAD_DIM), F32)
            e = 0
            for h, first, last in items:
                count = last - first
                q = jnp.concatenate(
                    [q_all[b, :, (h * grp + g) * HEAD_DIM:(h * grp + g + 1) * HEAD_DIM]
                     for g in range(first, last)], axis=0)
                most = None
                for at, size in spans:
                    s = lax.dot_general(
                        q, kbuf[at:at + size, h * HEAD_DIM:(h + 1) * HEAD_DIM],
                        (((1,), (1,)), ((), ())), preferred_element_type=F32)
                    s = (s.reshape(count, rows, size) + bias[:, at:at + size][None]).reshape(count * rows, size)
                    s_scr[slot, :, at:at + size] = s
                    for j in range(0, size, HEAD_DIM):
                        piece = s[:, j:j + HEAD_DIM]
                        most = piece if most is None else jnp.maximum(most, piece)
                top = jnp.max(most, axis=1, keepdims=True)
                shift = top * scale2
                acc = None
                for at, size in spans:
                    p = jnp.exp2(s_scr[slot, :, at:at + size] * scale2 - shift).astype(BF16)
                    term = jnp.dot(p, vbuf[h, at:at + size, :], preferred_element_type=F32)
                    acc = term if acc is None else acc + term
                total = acc[:, HEAD_DIM:]
                value = (acc[:, :HEAD_DIM] / jnp.maximum(total, 1.0)).astype(BF16)
                lse = jnp.where(top > 0.5 * NEG, top * scale + jnp.log(jnp.maximum(total, 1.0)), NEG)
                for g in range(count):
                    part[b, side, :, e * HEAD_DIM:(e + 1) * HEAD_DIM] = value[g * rows:(g + 1) * rows]
                    for r in range(bands):
                        packed = jnp.where(
                            band_lane == r * heads + e, lse[g * rows + r * 8:g * rows + r * 8 + 8], packed)
                    e += 1
                slot += 1
            stat[b, side] = packed

        mate_stat(b).start()
        mate_part(b).start()

        @pl.when(lax.rem(i, 2) == 1)
        def _():
            combine(b)
            combine(block_of(i - 1))
        return 0

    lax.fori_loop(0, n, step, 0)

    def close(j, _):
        conclude(block_of(n - 1 - j))
        return 0

    lax.fori_loop(0, n, close, 0)

    everyone = n * rows
    pick = (lax.broadcasted_iota(jnp.int32, (everyone, everyone), 0) == rd_ref[...]).astype(F32).astype(BF16)

    def arrange(side):
        for at, size in tiles_of(half, 1024):
            order[:, pl.ds(pl.multiple_of(side * half + at, HEAD_DIM), size)] = jnp.dot(
                pick, att[:, side, :, at:at + size].reshape(everyone, size),
                preferred_element_type=F32).astype(BF16)

    arrange(core)
    for b in range(n):
        att_part(b, 1 - core).wait_recv()
    arrange(1 - core)

    def columns(c):
        return pl.ds(pl.multiple_of(c * cw, cw), cw)

    def share(t):
        return pl.ds(t * orows, orows)

    def up(c, t):
        return pltpu.make_async_remote_copy(
            src_ref=ybuf.at[share(t), columns(c)], dst_ref=rbuf.at[t, :, columns(c)],
            send_sem=y_send.at[t, c], recv_sem=y_recv.at[t, c],
            device_id={"head": above}, device_id_type=MESH)

    def down(c, t):
        slot = jnp.where(hz - 1 == t, nh, t)
        return pltpu.make_async_remote_copy(
            src_ref=ybuf.at[share(t), columns(c)], dst_ref=rbuf.at[slot, :, columns(c)],
            send_sem=y_send.at[t, c], recv_sem=y_recv.at[slot, c],
            device_id={"head": below}, device_id_type=MESH)

    def arrived(c, slot):
        return pltpu.make_async_remote_copy(
            src_ref=rbuf.at[slot, :, columns(c)], dst_ref=rbuf.at[slot, :, columns(c)],
            send_sem=y_send.at[slot, c], recv_sem=y_recv.at[slot, c],
            device_id={"head": above}, device_id_type=MESH)

    def add_arrived(c, t):
        arrived(c, t).wait_recv()
        cols = columns(c)
        ybuf[share(t), cols] = (ybuf[share(t), cols].astype(F32) + rbuf[t, :, cols].astype(F32)).astype(BF16)

    def project(k, _):
        @pl.when(k < chunks)
        def _():
            wcopy(k).wait()
            ybuf[:, columns(k)] = jnp.dot(
                order[...], wbuf[k], preferred_element_type=F32).astype(BF16)

        rise = k - hz
        fall = k - (nh - 1 - hz)
        for t in reversed(range(1, nh)):
            @pl.when((rise >= 0) & (rise < chunks) & (hz == 0) & (t > 1))
            def _():
                up(rise, t).start()

            @pl.when((rise >= 0) & (rise < chunks) & (hz > 0) & (t > hz))
            def _():
                add_arrived(rise, t)
                up(rise, t).start()

        for t in range(nh - 1):
            @pl.when((fall >= 0) & (fall < chunks) & (hz == nh - 1) & (t < nh - 2))
            def _():
                down(fall, t).start()

            @pl.when((fall >= 0) & (fall < chunks) & (hz < nh - 1) & (t < hz))
            def _():
                add_arrived(fall, t)
                down(fall, t).start()

        @pl.when(k == chunks - 1)
        def _():
            def near(c, _):
                @pl.when(hz == 0)
                def _():
                    up(c, 1).start()

                @pl.when(hz == nh - 1)
                def _():
                    down(c, nh - 2).start()
                return 0

            lax.fori_loop(0, chunks, near, 0)
        return 0

    lax.fori_loop(0, chunks + nh - 2, project, 0)

    def leave(c):
        return pltpu.make_async_copy(obuf.at[:, columns(c)], out_ref.at[:, columns(c)], o_sem.at[c])

    def finish(c, _):
        cols = columns(c)
        mine = pl.ds(pl.multiple_of(hz * orows, orows), orows)

        @pl.when(hz == 0)
        def _():
            arrived(c, nh).wait_recv()
            obuf[:, cols] = (ybuf[mine, cols].astype(F32) + rbuf[nh, :, cols].astype(F32)).astype(BF16)

        @pl.when(hz == nh - 1)
        def _():
            arrived(c, hz).wait_recv()
            obuf[:, cols] = (ybuf[mine, cols].astype(F32) + rbuf[hz, :, cols].astype(F32)).astype(BF16)

        @pl.when((hz > 0) & (hz < nh - 1))
        def _():
            arrived(c, hz).wait_recv()
            arrived(c, nh).wait_recv()
            obuf[:, cols] = (ybuf[mine, cols].astype(F32) + rbuf[hz, :, cols].astype(F32)
                             + rbuf[nh, :, cols].astype(F32)).astype(BF16)

        leave(c).start()
        return 0

    lax.fori_loop(0, chunks, finish, 0)

    for k in range(1, chips):
        q_out(k).wait_send()
        q_pass(jnp.int32(2 * k)).wait_send()
    q_mate.wait_send()

    def drain(b, _):
        mate_stat(b).wait_send()
        mate_part(b).wait_send()
        att_part(b, core).wait_send()
        for d in range(1, chips):
            chip_stat(b, d).wait_send()
            chip_part(b, d).wait_send()
        return 0

    lax.fori_loop(0, n, drain, 0)

    def drain_y(c, _):
        for t in range(nh):
            @pl.when(t != hz)
            def _():
                up(c, t).wait_send()
        leave(c).wait()
        return 0

    lax.fori_loop(0, chunks, drain_y, 0)


def per_device(
    n, nh, queries, cache_keys, cache_values, new_keys, new_values, out_weight,
    new_counts, cache_counts, row_dest,
):
    rows, width = queries.shape
    cached, kvw = cache_keys.shape
    kv = kvw // HEAD_DIM
    grp = width // kvw
    depth, cols = out_weight.shape
    keys = cached * 3 // 4 + -(-rows // HEAD_DIM) * HEAD_DIM
    everyone = n * rows
    orows = everyone // nh
    chips = n // 2
    half = width // 2
    plan = parts_of(kv, grp)
    slots = sum(len(items) for items in plan)
    tall = (plan[0][0][2] - plan[0][0][1]) * rows
    cw = 1024 if cols % 1024 == 0 else HEAD_DIM
    chunks = cols // cw
    dma = pltpu.SemaphoreType.DMA
    hbm = pl.BlockSpec(memory_space=pl.ANY)
    smem = pl.BlockSpec(memory_space=pltpu.SMEM)
    vmem = pl.BlockSpec(memory_space=pltpu.VMEM)
    return pl.pallas_call(
        functools.partial(fused, n, nh),
        out_shape=jax.ShapeDtypeStruct((orows, cols), BF16),
        in_specs=[hbm] * 6 + [smem] * 2 + [vmem],
        out_specs=hbm,
        scratch_shapes=[
            pltpu.VMEM((n, rows, width), BF16),
            pltpu.VMEM((keys, kvw), BF16),
            pltpu.VMEM((kv, keys, 2 * HEAD_DIM), BF16),
            pltpu.VMEM((rows, keys), F32),
            pltpu.VMEM((slots, tall, keys), F32),
            pltpu.VMEM((n, 2, rows, half), BF16),
            pltpu.VMEM((n, 2, 8, HEAD_DIM), F32),
            pltpu.VMEM((n, rows, half), BF16),
            pltpu.VMEM((n, 8, HEAD_DIM), F32),
            pltpu.VMEM((n, rows, half), BF16),
            pltpu.VMEM((n, 8, HEAD_DIM), F32),
            pltpu.VMEM((chips - 1, n, rows, half), BF16),
            pltpu.VMEM((chips - 1, n, 8, HEAD_DIM), F32),
            pltpu.VMEM((n, 2, rows, half), BF16),
            pltpu.VMEM((everyone, width), BF16),
            pltpu.VMEM((chunks, depth, cw), BF16),
            pltpu.VMEM((everyone, cols), BF16),
            pltpu.VMEM((nh + 1, orows, cols), BF16),
            pltpu.VMEM((orows, cols), BF16),
            dma((2,)), dma((kv, 2)), dma((chunks,)), dma,
            dma((n,)), dma((n,)),
            dma((n,)), dma((n,)), dma((n,)), dma((n,)),
            dma((chips - 1, n)), dma((chips - 1, n)), dma((chips - 1, n)), dma((chips - 1, n)),
            dma((n,)), dma((n,)),
            dma((nh + 1, chunks)), dma((nh + 1, chunks)), dma((chunks,)),
        ],
        compiler_params=pltpu.CompilerParams(
            collective_id=0, has_side_effects=True, vmem_limit_bytes=60 * 1024 * 1024),
    )(queries, cache_keys, cache_values, new_keys, new_values, out_weight,
      new_counts, cache_counts, row_dest.reshape(1, everyone))


def solution(mesh):
    n, nh = mesh.shape["ctx"], mesh.shape["head"]
    return jax.shard_map(
        functools.partial(per_device, n, nh),
        mesh=mesh,
        in_specs=(
            P(("groups", "ctx"), "head"),
            P(("groups", "ctx"), "head"),
            P(("groups", "ctx"), "head"),
            P(("groups", "ctx"), "head"),
            P(("groups", "ctx"), "head"),
            P("head", "ctx"),
            P("groups", None),
            P("groups", None),
            P("groups"),
        ),
        out_specs=P(("groups", "head"), "ctx"),
        check_vma=False,
    )
```

time: 59.3 us -> 50.2 us (0.85)
  Pallas kernels: 57.5 us -> 48.4 us
    pallas_call x1, Pallas kernels: 57.5 us -> 48.4 us  [per_device(): pl.pallas_call(functools.partial(fused, n, nh), out_shape=jax.ShapeDtypeS...]
where the time goes in v1:
time: 50.2 us; the launch traced here: 50 us
  Pallas kernels  48.4 us (96%)
  local copies, waits for them, and re-layouts  1.67 us (3%)
    pallas_call x1, Pallas kernels, per_device(): pl.pallas_call(functools.partial(fused, n, nh), out_shape=jax.ShapeDtypeS...  48.4 us
    unnamed x1, local copies, waits for them, and re-layouts  1.67 us

profile of v1, /device:TPU:0, one launch (start us, length us, event | category | flops | bytes accessed | tf_op | source)
XLA Modules:
  0.0 50.0 jit_solution(15802415740779463777)
XLA Ops:
  0.0 48.4 %shard_map.91 = bf16[32,4096]{1,0:T(8,128)(2,1)} custom-call(bf16[32,4096]{1,0:T(8,128)(2,1)} %q_ref.1, bf16[2048,256]{1,0:T(8,128)(2,1)} %ck_ref.1, bf16[2048,256]{1,0:T(8,128)(2,1)} %cv_ref.1, bf16[32,256]{1,0:T(8,128)(2,1)} %nk_ref.1, bf16[32,256]{1,0:T(8,128)(2,1)} %nv_ref.1, bf16[4096,4096]{1,0:T(8,128)(2,1)} %w_ref.1, s32[4,4]{1,0:T(4,128)} %ncnt.1, ...), custom_call_target="tpu_custom_call" | custom-call | tf_op jit(solution)/shard_map/pallas_call | solution.py:454
  48.4 1.7 %copy.11 = bf16[32,4096]{1,0:T(8,128)(2,1)} copy(bf16[32,4096]{1,0:T(8,128)(2,1)} %shard_map.91) | data formatting | bytes 524288

commit v2 on v1

--- a/solution.py
+++ b/solution.py
@@ -28,7 +28,7 @@
 def fused(
     n, nh, q_ref, ck_ref, cv_ref, nk_ref, nv_ref, w_ref, ncnt, ccnt, rd_ref, out_ref,
     q_all, kbuf, vbuf, bias, s_scr, part, stat, mpart, mstat, comb, cstat, xpart, xstat,
-    att, order, wbuf, ybuf, rbuf, obuf,
+    att, order, wbuf, start, ybuf, rbuf, obuf,
     k_sem, v_sem, w_sem, own_sem, q_send, q_recv, m_send, m_recv, ms_send, ms_recv,
     x_send, x_recv, xs_send, xs_recv, a_send, a_recv, y_send, y_recv, o_sem,
 ):
@@ -164,21 +164,26 @@
     def att_part(b, side):
         return to_ctx(att.at[b, side], att.at[b, side], a_send.at[b], a_recv.at[b], mate)
 
+    band_lane = lax.broadcasted_iota(jnp.int32, (8, HEAD_DIM), 1)
+
     def spread(weight, e):
         return jnp.concatenate(
             [jnp.broadcast_to(weight[:, r * heads + e:r * heads + e + 1], (8, HEAD_DIM))
              for r in range(bands)], axis=0)
 
-    def blend(pieces, stats, store):
+    def blend(pieces, stats, store, last):
         best = functools.reduce(jnp.maximum, stats)
         weights = [jnp.exp(item - best) for item in stats]
-        whole = functools.reduce(jnp.add, weights)
-        weights = [item / whole for item in weights]
+        wide = [pltpu.roll(item, HEAD_DIM // 2, 1) for item in weights]
+        whole = functools.reduce(jnp.add, [w * item for w, item in zip(wide, stats)])
+        if last:
+            share = 1.0 / pltpu.roll(whole, HEAD_DIM // 2, 1)
+            weights = [item * share for item in weights]
         for e in range(heads):
             cols = slice(e * HEAD_DIM, (e + 1) * HEAD_DIM)
             terms = [spread(w, e) * piece[:, cols].astype(F32) for w, piece in zip(weights, pieces)]
             store(cols, functools.reduce(jnp.add, terms).astype(BF16))
-        return best + jnp.log(whole)
+        return jnp.where(band_lane < HEAD_DIM // 2, best, whole)
 
     def combine(b):
         mate_stat(b).wait_recv()
@@ -187,7 +192,7 @@
         def store(cols, value):
             comb[b, :, cols] = value
 
-        cstat[b] = blend([part.at[b, core], mpart.at[b]], [stat[b, core], mstat[b]], store)
+        cstat[b] = blend([part.at[b, core], mpart.at[b]], [stat[b, core], mstat[b]], store, False)
         for d in range(1, chips):
             chip_stat(b, d).start()
             chip_part(b, d).start()
@@ -201,11 +206,10 @@
             att[b, core, :, cols] = value
 
         blend([comb.at[b]] + [xpart.at[d - 1, b] for d in range(1, chips)],
-              [cstat[b]] + [xstat[d - 1, b] for d in range(1, chips)], store)
+              [cstat[b]] + [xstat[d - 1, b] for d in range(1, chips)], store, True)
         att_part(b, core).start()
 
     spans = tiles_of(keys, 512)
-    band_lane = lax.broadcasted_iota(jnp.int32, (8, HEAD_DIM), 1)
 
     def step(i, _):
         b = block_of(i)
@@ -254,16 +258,17 @@
                     term = jnp.dot(p, vbuf[h, at:at + size, :], preferred_element_type=F32)
                     acc = term if acc is None else acc + term
                 total = acc[:, HEAD_DIM:]
-                value = (acc[:, :HEAD_DIM] / jnp.maximum(total, 1.0)).astype(BF16)
-                lse = jnp.where(top > 0.5 * NEG, top * scale + jnp.log(jnp.maximum(total, 1.0)), NEG)
+                value = acc[:, :HEAD_DIM].astype(BF16)
+                most = jnp.broadcast_to(top, (count * rows, HEAD_DIM))
                 for g in range(count):
                     part[b, side, :, e * HEAD_DIM:(e + 1) * HEAD_DIM] = value[g * rows:(g + 1) * rows]
                     for r in range(bands):
-                        packed = jnp.where(
-                            band_lane == r * heads + e, lse[g * rows + r * 8:g * rows + r * 8 + 8], packed)
+                        band = slice(g * rows + r * 8, g * rows + r * 8 + 8)
+                        packed = jnp.where(band_lane == r * heads + e, most[band], packed)
+                        packed = jnp.where(band_lane == HEAD_DIM // 2 + r * heads + e, total[band], packed)
                     e += 1
                 slot += 1
-            stat[b, side] = packed
+            stat[b, side] = jnp.where(band_lane < HEAD_DIM // 2, packed * scale, packed)
 
         mate_stat(b).start()
         mate_part(b).start()
@@ -291,10 +296,17 @@
                 pick, att[:, side, :, at:at + size].reshape(everyone, size),
                 preferred_element_type=F32).astype(BF16)
 
+    def first_chunk(side):
+        at = pl.ds(pl.multiple_of(side * half, HEAD_DIM), half)
+        return jnp.dot(order[:, at], wbuf[0, at, :], preferred_element_type=F32)
+
     arrange(core)
+    wcopy(0).wait()
+    start[...] = first_chunk(core)
     for b in range(n):
         att_part(b, 1 - core).wait_recv()
     arrange(1 - core)
+    ybuf[:, pl.ds(0, cw)] = (start[...] + first_chunk(1 - core)).astype(BF16)
 
     def columns(c):
         return pl.ds(pl.multiple_of(c * cw, cw), cw)
@@ -327,7 +339,7 @@
         ybuf[share(t), cols] = (ybuf[share(t), cols].astype(F32) + rbuf[t, :, cols].astype(F32)).astype(BF16)
 
     def project(k, _):
-        @pl.when(k < chunks)
+        @pl.when((k > 0) & (k < chunks))
         def _():
             wcopy(k).wait()
             ybuf[:, columns(k)] = jnp.dot(
@@ -473,6 +485,7 @@
             pltpu.VMEM((n, 2, rows, half), BF16),
             pltpu.VMEM((everyone, width), BF16),
             pltpu.VMEM((chunks, depth, cw), BF16),
+            pltpu.VMEM((everyone, cw), F32),
             pltpu.VMEM((everyone, cols), BF16),
             pltpu.VMEM((nh + 1, orows, cols), BF16),
             pltpu.VMEM((orows, cols), BF16),

time: 50.2 us -> 50.4 us (level)
  no operation moved by 1% of the time
where the time goes in v2:
time: 50.4 us; the launch traced here: 50.2 us
  Pallas kernels  48.5 us (96%)
  local copies, waits for them, and re-layouts  1.67 us (3%)
    pallas_call x1, Pallas kernels, per_device(): pl.pallas_call(functools.partial(fused, n, nh), out_shape=jax.ShapeDtypeS...  48.5 us
    unnamed x1, local copies, waits for them, and re-layouts  1.67 us

profile of v2, /device:TPU:0, one launch (start us, length us, event | category | flops | bytes accessed | tf_op | source)
XLA Modules:
  0.0 50.2 jit_solution(505960413264463552)
XLA Ops:
  0.0 48.5 %shard_map.91 = bf16[32,4096]{1,0:T(8,128)(2,1)} custom-call(bf16[32,4096]{1,0:T(8,128)(2,1)} %q_ref.1, bf16[2048,256]{1,0:T(8,128)(2,1)} %ck_ref.1, bf16[2048,256]{1,0:T(8,128)(2,1)} %cv_ref.1, bf16[32,256]{1,0:T(8,128)(2,1)} %nk_ref.1, bf16[32,256]{1,0:T(8,128)(2,1)} %nv_ref.1, bf16[4096,4096]{1,0:T(8,128)(2,1)} %w_ref.1, s32[4,4]{1,0:T(4,128)} %ncnt.1, ...), custom_call_target="tpu_custom_call" | custom-call | tf_op jit(solution)/shard_map/pallas_call | solution.py:466
  48.5 1.7 %copy.11 = bf16[32,4096]{1,0:T(8,128)(2,1)} copy(bf16[32,4096]{1,0:T(8,128)(2,1)} %shard_map.91) | data formatting | bytes 524288
